TPU v7x, 256 devices: a whole 4x4x8 slice. The times are simulated.
256 devices in a mesh: req: 32 (over y, x, z_hi), tp: 8 (over z_lo, core).
Axes of the slice: x: 4, y: 4, z: 8 (z_hi: 2, z_lo: 4; z = z_hi * 4 + z_lo), core: 2. Of those that a mesh axis runs over, the one named last changes fastest.
Arguments:
- residual: bfloat16 [8192, 2304], P('req'), may hold values from -58 to 58
- context: bfloat16 [8192, 2304], P('req', 'tp'), may hold values from -6 to 6
- attention_output_weight: bfloat16 [2304, 2304], P('tp'), may hold values from -0.1875 to 0.1875
- adapter_down_maps: bfloat16 [64, 2304, 16], P('req', 'tp'), may hold values from -0.125 to 0.125
- adapter_up_maps: bfloat16 [64, 16, 2304], P('req'), may hold values from -1.5 to 1.5
- adapter_storage_row: int32 [64], replicated, may hold values from 0 to 63, each once
- active_adapters: int32 [16], replicated, may hold values from 0 to 63, as said below
- request_token_length: int32 [32, 4], P('req'), may hold values from 1 to 128, 256 in all within a row
- request_adapter_entry: int32 [32, 4], P('req'), may hold values from 0 to 15
- expert_norm_gain: bfloat16 [2304], replicated, may hold values from 0.099609375 to 1.8984375
- router_projection: bfloat16 [2304, 8], replicated, may hold values from -0.125 to 0.125
- expert_choice_pairs: int32 [8192, 2], P('req'), may hold values from 0 to 7, all different within a row; in each aligned block of 256 rows (0 to 255, 256 to 511, ...) at most 80 rows name the same one
- expert_gate_weight: bfloat16 [32, 2304, 5760], P('req', None, 'tp'), as said below
- expert_up_weight: bfloat16 [32, 2304, 5760], P('req', None, 'tp'), as said below
- expert_down_weight: bfloat16 [32, 5760, 2304], P('req', 'tp'), as said below
Outputs:
- layer_out: bfloat16 [8192, 2304], P('req', 'tp')
Inputs may be any that keep to these rules, and one draw needn't show every extreme that they name: `active_adapters`: 16 different adapter numbers, 0 and 63 among them. `adapter_storage_row`: every stored row appears once. `request_token_length`: each group's lengths sum to 256; the longest request of a group has exactly half of 256 tokens. `expert_choice_pairs`: each row names two different experts; within the 256 rows of one group no expert is named by more than 80 rows, a bound that some block reaches. `expert_gate_weight`: the 4 holders c * 8 + e of expert e hold the same weights. `expert_up_weight`: the 4 holders c * 8 + e of expert e hold the same weights. `expert_down_weight`: the 4 holders c * 8 + e of expert e hold the same weights.
All inputs are finite; a program needn't handle non-finite values.
Results may differ from a plain program's by a relative error of at most 0.0095.
Values may be sent and summed in bfloat16 or wider, within the bound.
A program may use at most 128 MiB of HBM per device.

v0:
```python
import jax
import jax.numpy as jnp
from jax import lax
from jax.sharding import Mesh
from jax.sharding import PartitionSpec as P

CAP = 80
NORM_EPS = 1e-05
REQ = ("ry", "rxz")


def segment_onehot(request_token_length, token_count):
    bounds = jnp.cumsum(request_token_length[0])
    position = jnp.arange(token_count, dtype=jnp.int32)
    segment = jnp.sum((position[:, None] >= bounds[None, :]).astype(jnp.int32), axis=1)
    slot_range = jnp.arange(request_token_length.shape[1], dtype=jnp.int32)
    return segment[:, None] == slot_range[None, :]


def route_tables(expert_choice_pairs, expert_count, capacity):
    expert_ids = jnp.arange(expert_count, dtype=jnp.int32)
    first_hit = expert_choice_pairs[None, :, 0] == expert_ids[:, None]
    second_hit = expert_choice_pairs[None, :, 1] == expert_ids[:, None]
    chosen = first_hit | second_hit
    slot_of = jnp.cumsum(chosen.astype(jnp.int32), axis=1) - 1
    slot_range = jnp.arange(capacity, dtype=jnp.int32)
    placement = chosen[:, None, :] & (slot_of[:, None, :] == slot_range[None, :, None])
    return (placement, first_hit, second_hit)


def on_device(
    residual,
    context,
    attention_output_weight,
    adapter_down_maps,
    adapter_up_maps,
    adapter_storage_row,
    active_adapters,
    request_token_length,
    request_adapter_entry,
    expert_norm_gain,
    router_projection,
    expert_choice_pairs,
    expert_gate_weight,
    expert_up_weight,
    expert_down_weight,
):
    token_count = residual.shape[0]
    hidden_width = residual.shape[1]
    feature_share = context.shape[1]
    local_rows = adapter_down_maps.shape[0]
    adapter_rank_size = adapter_down_maps.shape[2]
    request_count = request_token_length.shape[1]
    share_width = hidden_width // lax.axis_size("tp")
    share_start = lax.axis_index("tp") * share_width
    up_slice = lax.dynamic_slice_in_dim(adapter_up_maps, share_start, share_width, 2)
    packed = jnp.concatenate(
        [
            adapter_down_maps.reshape(local_rows, feature_share * adapter_rank_size),
            up_slice.reshape(local_rows, adapter_rank_size * share_width),
        ],
        axis=1,
    )
    all_packed = lax.all_gather(packed, REQ, axis=0, tiled=True)
    request_rows = adapter_storage_row[active_adapters[request_adapter_entry[0]]]
    picked = all_packed[request_rows]
    down_req = picked[:, : feature_share * adapter_rank_size].reshape(
        request_count, feature_share, adapter_rank_size
    )
    up_req = picked[:, feature_share * adapter_rank_size :].reshape(
        request_count * adapter_rank_size, share_width
    )
    down_joined = jnp.transpose(down_req, (1, 0, 2)).reshape(
        feature_share, request_count * adapter_rank_size
    )
    segment_hot = segment_onehot(request_token_length, token_count)
    low_all = jnp.dot(context, down_joined, preferred_element_type=jnp.float32)
    reduced_mask = jnp.repeat(segment_hot, adapter_rank_size, axis=1)
    low_part = jnp.where(reduced_mask, low_all, 0.0)
    low_total = lax.psum(low_part, "tp").astype(jnp.bfloat16)
    lora_share = jnp.dot(low_total, up_req, preferred_element_type=jnp.float32)
    base = jnp.dot(context, attention_output_weight, preferred_element_type=jnp.float32)
    base_share = lax.dynamic_slice_in_dim(base, share_start, share_width, 1)
    head_part = lax.dynamic_update_slice_in_dim(base, base_share + lora_share, share_start, 1)
    gain_all = expert_norm_gain.astype(jnp.float32)
    head_sum = lax.psum(head_part.astype(jnp.bfloat16), "tp").astype(jnp.float32)
    blended_rows = residual.astype(jnp.float32) + head_sum
    mean_square = jnp.mean(blended_rows * blended_rows, axis=1, keepdims=True)
    normed = (blended_rows * lax.rsqrt(mean_square + NORM_EPS) * gain_all).astype(jnp.bfloat16)
    mixed_share = lax.dynamic_slice_in_dim(blended_rows, share_start, share_width, 1)
    logits = jnp.dot(normed, router_projection, preferred_element_type=jnp.float32)
    expert_count = router_projection.shape[1]
    expert_range = jnp.arange(expert_count, dtype=jnp.int32)
    logit_first = jnp.sum(
        jnp.where(expert_choice_pairs[:, 0:1] == expert_range[None, :], logits, 0.0), axis=1
    )
    logit_second = jnp.sum(
        jnp.where(expert_choice_pairs[:, 1:2] == expert_range[None, :], logits, 0.0), axis=1
    )
    weight_first = 1.0 / (1.0 + jnp.exp(logit_second - logit_first))
    weight_second = 1.0 / (1.0 + jnp.exp(logit_first - logit_second))
    placement, first_hit, second_hit = route_tables(expert_choice_pairs, expert_count, CAP)
    send_rows = jnp.einsum(
        "est,td->esd", placement.astype(jnp.bfloat16), normed, preferred_element_type=jnp.float32
    ).astype(jnp.bfloat16)
    rows_in = lax.all_to_all(send_rows, "rxz", split_axis=0, concat_axis=0, tiled=True)
    rows_flat = rows_in.reshape(expert_count * CAP, hidden_width)
    gate_value = jnp.dot(rows_flat, expert_gate_weight[0], preferred_element_type=jnp.float32)
    up_value = jnp.dot(rows_flat, expert_up_weight[0], preferred_element_type=jnp.float32)
    hidden = (jax.nn.silu(gate_value) * up_value).astype(jnp.bfloat16)
    partial_value = jnp.dot(hidden, expert_down_weight[0], preferred_element_type=jnp.float32)
    returned = lax.all_to_all(
        partial_value.astype(jnp.bfloat16).reshape(expert_count, CAP, hidden_width),
        "rxz",
        split_axis=0,
        concat_axis=0,
        tiled=True,
    )
    token_weight = jnp.where(first_hit, weight_first[None, :], 0.0) + jnp.where(
        second_hit, weight_second[None, :], 0.0
    )
    scaled_place = placement.astype(jnp.float32) * token_weight[:, None, :]
    contribution = jnp.einsum(
        "est,esd->td",
        scaled_place,
        returned.astype(jnp.float32),
        precision=lax.Precision.HIGHEST,
        preferred_element_type=jnp.float32,
    )
    moe_share = lax.psum_scatter(
        contribution.astype(jnp.bfloat16), "tp", scatter_dimension=1, tiled=True
    ).astype(jnp.float32)
    return (mixed_share + moe_share).astype(jnp.bfloat16)


def solution(mesh):
    req_size = mesh.shape["req"]
    plane = 8
    split_mesh = Mesh(
        mesh.devices.reshape(req_size // plane, plane, mesh.shape["tp"]), ("ry", "rxz", "tp")
    )
    return jax.shard_map(
        on_device,
        mesh=split_mesh,
        in_specs=(
            P(REQ, None),
            P(REQ, "tp"),
            P("tp", None),
            P(REQ, "tp", None),
            P(REQ, None, None),
            P(),
            P(),
            P(REQ, None),
            P(REQ, None),
            P(),
            P(),
            P(REQ, None),
            P(REQ, None, "tp"),
            P(REQ, None, "tp"),
            P(REQ, "tp", None),
        ),
        out_specs=P(REQ, "tp"),
        check_vma=False,
    )
```

profile of v0, /device:TPU:4, one launch (start us, length us, event | category | flops | bytes accessed | tf_op | source)
XLA Modules:
  0.0 434.4 jit_solution(16234100951384589022)
XLA Ops:
  13.6 3.6 fusion.35
  17.2 77.7 %all-gather.3.cloned.1.call-done = bf16[32,2,9216]{2,1,0:T(2,128)(2,1)} async-done(((bf16[1,2,9216]{2,1,0:T(2,128)(2,1)}), bf16[32,2,9216]{2,1,0:T(2,128)(2,1)}) %all-gather.3.cloned.1.call-update) | async-done | bytes 1179664 | tf_op jit(solution)/shard_map/all_gather | solution.py:64
  94.9 2.3 reshape.300
  97.3 2.1 gather_fusion.2
  100.0 1.5 reshape.271
  101.5 1.7 reshape.269
  103.3 1.7 copy.30
  106.0 26.3 %psum.14 = bf16[256,64]{0,1:T(8,128)(2,1)S(1)} all-reduce(f32[256,64]{0,1:T(8,128)S(1)} %fusion.10), channel_id=1, replica_groups=mesh['ry'=4,'rxz'=8,'tp'=8] {'tp'}, use_global_device_ids=true, to_apply=%region_2.3 | all-reduce | flops 16384 | bytes 98304 | tf_op jit(solution)/shard_map/psum | solution.py:80
  132.3 2.1 convolution_add_fusion
  134.4 3.5 dynamic_update_slice.3
  137.9 2.8 convert_element_type.49
  141.7 69.1 %all-reduce.2.cloned.1.call-done = bf16[256,2304]{1,0:T(8,128)(2,1)} async-done(((bf16[256,2304]{1,0:T(8,128)(2,1)}), bf16[256,2304]{1,0:T(8,128)(2,1)}) %all-reduce.2.cloned.1.call-update) | async-done | bytes 1179664 | tf_op jit(solution)/shard_map/psum | solution.py:86
  210.8 3.6 convert_add_fusion
  215.6 74.4 %all_to_all.10 = bf16[8,80,2304]{2,1,0:T(8,128)(2,1)S(1)} all-to-all(bf16[8,80,2304]{2,1,0:T(8,128)(2,1)S(1)} %convolution_convert_fusion.1), channel_id=1, replica_groups=mesh['ry'=4,'rxz'=8,'tp'=8] {'rxz'}, dimensions={0} | all-to-all | bytes 5898240 | tf_op jit(solution)/shard_map/all_to_all | solution.py:106
  290.0 1.6 copy-done.3
  291.7 4.0 fusion.5
  295.6 14.5 %convolution_convert_fusion = bf16[640,2304]{1,0:T(8,128)(2,1)} fusion(bf16[1,720,2304]{2,1,0:T(8,128)(2,1)S(1)} %copy-done, f32[640,720]{0,1:T(8,128)} %fusion.5, bf16[640,2304]{1,0:T(8,128)(2,1)} %bitcast.68, bf16[1,2304,720]{1,2,0:T(8,128)(2,1)} %param.28), kind=kOutput, calls=%fused_computation.3 | convolution fusion | flops 4250972160 | bytes 14376960 | tf_op jit(solution)/shard_map/dot_general | solution.py:111
  310.2 7.4 %all-to-all-start.1 = ((bf16[8,80,2304]{2,1,0:T(8,128)(2,1)}), bf16[8,80,2304]{2,1,0:T(8,128)(2,1)}, u32[]{:S(2)}, u32[]{:S(2)}) async-start(bf16[8,80,2304]{2,1,0:T(8,128)(2,1)} %bitcast.66), calls=%async_computation.1 | async-start | bytes 5898240 | tf_op jit(solution)/shard_map/all_to_all | solution.py:112
  317.5 2.2 select_reduce_fusion.1
  319.8 57.1 %all-to-all-done.1 = bf16[8,80,2304]{2,1,0:T(8,128)(2,1)} async-done(((bf16[8,80,2304]{2,1,0:T(8,128)(2,1)}), bf16[8,80,2304]{2,1,0:T(8,128)(2,1)}, u32[]{:S(2)}, u32[]{:S(2)}) %all-to-all-start.1) | async-done | bytes 2949152 | tf_op jit(solution)/shard_map/all_to_all | solution.py:112
  376.9 6.4 %fusion.1 = bf16[2304,256]{1,0:T(8,128)(2,1)} fusion(bf16[8,80,2304]{2,1,0:T(8,128)(2,1)} %all-to-all-done.1, f32[8,256]{1,0:T(8,128)S(1)} %select_add_fusion, s32[8,256]{1,0:T(8,128)S(1)} %add_bitcast_fusion, pred[8,256]{1,0:T(8,128)(4,1)S(1)} %fusion.24), kind=kOutput, calls=%fused_computation.7 | convolution fusion | flops 4530929664 | bytes 4147200 | tf_op jit(solution)/shard_map/est,esd->td/dot_general | solution.py:123
  383.3 39.9 %reduce-scatter.4.cloned.1.call-done = bf16[288,256]{1,0:T(8,128)(2,1)} async-done(((bf16[2304,256]{1,0:T(8,128)(2,1)}), bf16[288,256]{1,0:T(8,128)(2,1)}) %reduce-scatter.4.cloned.1.call-update) | async-done | bytes 147472
  424.3 1.9 add_convert_fusion
  426.2 1.7 copy.33
  (56 shorter events, 11.9 us)
Async XLA Ops:
  6.5 289.1 %copy-start = (bf16[1,720,2304]{2,1,0:T(8,128)(2,1)S(1)}, bf16[1,720,2304]{2,1,0:T(8,128)(2,1)}, u32[]{:S(2)}) copy-start(bf16[1,720,2304]{2,1,0:T(8,128)(2,1)} %param.29) | copy-start | bytes 9953284
  6.5 88.4 %all-gather.3.cloned.1.call-start = ((), (), s32[]{:S(2)}) async-start(), calls=%async_computation.4 | async-start | bytes 1216512 | tf_op jit(solution)/shard_map/all_gather | solution.py:64
  9.4 201.5 %all-reduce.2.cloned.1.call-start = ((), (), s32[]{:S(2)}) async-start(), calls=%async_computation.3 | async-start | bytes 2359296 | tf_op jit(solution)/shard_map/psum | solution.py:86
  17.2 87.8 %copy-start.4 = (bf16[256,288]{0,1:T(8,128)(2,1)S(1)}, bf16[256,288]{0,1:T(8,128)(2,1)}, u32[]{:S(2)}) copy-start(bf16[256,288]{0,1:T(8,128)(2,1)} %param.16) | copy-start | bytes 442372
  137.9 2.8 copy-start.6
  137.9 3.7 copy-start.5
  210.8 3.6 copy-start.1
  210.8 3.6 copy-start.2
  215.6 76.1 %copy-start.7 = (bf16[1,2304,720]{1,2,0:T(8,128)(2,1)S(1)}, bf16[1,2304,720]{1,2,0:T(8,128)(2,1)}, u32[]{:S(2)}) copy-start(bf16[1,2304,720]{1,2,0:T(8,128)(2,1)} %param.27) | copy-start | bytes 9953284
  290.0 1.6 copy-start.3
  310.1 7.4 %copy-start.8 = (bf16[2304,8]{0,1:T(8,128)(2,1)S(1)}, bf16[2304,8]{0,1:T(8,128)(2,1)}, u32[]{:S(2)}) copy-start(bf16[2304,8]{0,1:T(8,128)(2,1)} %param.25) | copy-start | bytes 110596
  310.2 66.7 %all-to-all-start.1 = ((bf16[8,80,2304]{2,1,0:T(8,128)(2,1)}), bf16[8,80,2304]{2,1,0:T(8,128)(2,1)}, u32[]{:S(2)}, u32[]{:S(2)}) async-start(bf16[8,80,2304]{2,1,0:T(8,128)(2,1)} %bitcast.66), calls=%async_computation.1 | async-start | bytes 5898240 | tf_op jit(solution)/shard_map/all_to_all | solution.py:112
  317.5 105.7 %reduce-scatter.4.cloned.1.call-start = ((), (), s32[]{:S(2)}) async-start(), calls=%async_computation.5 | async-start | bytes 1327104
Sparse Core Ops, SparseCore 0:
  10.8 84.0 all-gather.2
  140.8 69.9 all-reduce.1
  383.4 39.7 reduce-scatter.3
where the time goes:
time: 435 us; the launch traced here: 434 us
  waiting for transfers between devices  244 us (56%)
  blocking collectives  101 us (23%)
  matrix products  34.9 us (8%)
  local copies, waits for them, and re-layouts  22.9 us (5%)
  between operations  13.2 us (3%)
  other arithmetic  11.3 us (3%)
  starting transfers between devices  7.41 us (2%)
    all_gather x1, waiting for transfers between devices, on_device(): all_packed = lax.all_gather(packed, REQ, axis=0, tiled=True)  77.7 us
    all_to_all x1, blocking collectives, on_device(): lax.all_to_all(send_rows, 'rxz', split_axis=0, concat_axis=0, tiled=True)  74.4 us
    psum x1, waiting for transfers between devices, on_device(): lax.psum(head_part.astype(jnp.bfloat16), 'tp').astype(jnp.float32)  69.1 us
    all_to_all x1, waiting for transfers between devices, on_device(): lax.all_to_all(partial_value.astype(jnp.bfloat16).reshape(expert_count, C...  57.1 us
    unnamed x4, waiting for transfers between devices  40 us
    psum x1, blocking collectives, on_device(): low_total = lax.psum(low_part, 'tp').astype(jnp.bfloat16)  26.3 us
    dot_general x1, matrix products, on_device(): jnp.dot(hidden, expert_down_weight[0], preferred_element_type=jnp.float32)  14.5 us
  transfers between devices with their start and end apart: 4, of which 4 were waited for; matrix products, arithmetic and copies ran while one was open for 3% of the time, Pallas kernels for 0%

commit v1 on v0

--- a/solution.py
+++ b/solution.py
@@ -61,7 +61,9 @@
         ],
         axis=1,
     )
-    all_packed = lax.all_gather(packed, REQ, axis=0, tiled=True)
+    all_packed = jnp.concatenate(
+        lax.all_to_all(jnp.stack([packed] * lax.axis_size(REQ)), REQ, 0, 0), axis=0
+    )
     request_rows = adapter_storage_row[active_adapters[request_adapter_entry[0]]]
     picked = all_packed[request_rows]
     down_req = picked[:, : feature_share * adapter_rank_size].reshape(

time: 435 us -> 397 us (0.913)
  waiting for transfers between devices: 244 us -> 192 us
  starting transfers between devices: 7.41 us -> 21.7 us
    all_gather x1 -> x0, waiting for transfers between devices: 77.7 us -> none  [on_device(): all_packed = lax.all_gather(packed, REQ, axis=0, tiled=True)]
    all_to_all x0 -> x1, waiting for transfers between devices: none -> 24.9 us  [on_device(): lax.all_to_all(jnp.stack([packed] * lax.axis_size(REQ)), REQ, 0, 0)]
    all_to_all x0 -> x1, starting transfers between devices: none -> 14.3 us  [on_device(): lax.all_to_all(jnp.stack([packed] * lax.axis_size(REQ)), REQ, 0, 0)]
    unnamed x4 -> x3, waiting for transfers between devices: 40 us -> 39.9 us
  transfers between devices with their start and end apart: 4 -> 4, of which waited for: 4 -> 4; matrix products, arithmetic and copies ran while one was open for 3% -> 2% of each run, Pallas kernels for 0% -> 0%
where the time goes in v1:
time: 397 us; the launch traced here: 396 us
  waiting for transfers between devices  192 us (48%)
  blocking collectives  101 us (25%)
  matrix products  34.9 us (9%)
  local copies, waits for them, and re-layouts  23.3 us (6%)
  starting transfers between devices  21.7 us (5%)
  between operations  13.6 us (3%)
  other arithmetic  9.35 us (2%)
    all_to_all x1, blocking collectives, on_device(): lax.all_to_all(send_rows, 'rxz', split_axis=0, concat_axis=0, tiled=True)  74.4 us
    psum x1, waiting for transfers between devices, on_device(): lax.psum(head_part.astype(jnp.bfloat16), 'tp').astype(jnp.float32)  70.1 us
    all_to_all x1, waiting for transfers between devices, on_device(): lax.all_to_all(partial_value.astype(jnp.bfloat16).reshape(expert_count, C...  57.1 us
    unnamed x3, waiting for transfers between devices  39.9 us
    psum x1, blocking collectives, on_device(): low_total = lax.psum(low_part, 'tp').astype(jnp.bfloat16)  26.6 us
    all_to_all x1, waiting for transfers between devices, on_device(): lax.all_to_all(jnp.stack([packed] * lax.axis_size(REQ)), REQ, 0, 0)  24.9 us
    dot_general x1, matrix products, on_device(): jnp.dot(hidden, expert_down_weight[0], preferred_element_type=jnp.float32)  14.5 us
    all_to_all x1, starting transfers between devices, on_device(): lax.all_to_all(jnp.stack([packed] * lax.axis_size(REQ)), REQ, 0, 0)  14.3 us
  transfers between devices with their start and end apart: 4, of which 4 were waited for; matrix products, arithmetic and copies ran while one was open for 2% of the time, Pallas kernels for 0%

profile of v1, /device:TPU:4, one launch (start us, length us, event | category | flops | bytes accessed | tf_op | source)
XLA Modules:
  0.0 395.8 jit_solution(6382599815873459020)
XLA Ops:
  10.4 14.3 %all-to-all-start = ((bf16[32,2,9216]{2,1,0:T(2,128)(2,1)}), bf16[32,2,9216]{2,1,0:T(2,128)(2,1)}, u32[]{:S(2)}, u32[]{:S(2)}) async-start(bf16[32,2,9216]{2,1,0:T(2,128)(2,1)} %stack.2), calls=%async_computation | async-start | bytes 2359296 | tf_op jit(solution)/shard_map/all_to_all | solution.py:65
  26.3 3.5 fusion.35
  29.9 24.9 %all-to-all-done = bf16[32,2,9216]{2,1,0:T(2,128)(2,1)} async-done(((bf16[32,2,9216]{2,1,0:T(2,128)(2,1)}), bf16[32,2,9216]{2,1,0:T(2,128)(2,1)}, u32[]{:S(2)}, u32[]{:S(2)}) %all-to-all-start) | async-done | bytes 1179680 | tf_op jit(solution)/shard_map/all_to_all | solution.py:65
  54.7 2.3 reshape.274
  57.0 2.1 gather_fusion.2
  61.3 1.7 reshape.275
  63.0 1.7 copy.30
  65.7 26.6 %psum.14 = bf16[256,64]{0,1:T(8,128)(2,1)S(1)} all-reduce(f32[256,64]{0,1:T(8,128)S(1)} %fusion.10), channel_id=1, replica_groups=mesh['ry'=4,'rxz'=8,'tp'=8] {'tp'}, use_global_device_ids=true, to_apply=%region_2.3 | all-reduce | flops 16384 | bytes 98304 | tf_op jit(solution)/shard_map/psum | solution.py:82
  92.4 2.1 convolution_add_fusion
  94.4 3.5 dynamic_update_slice.3
  97.9 2.8 convert_element_type.49
  101.8 70.1 %all-reduce.2.cloned.1.call-done = bf16[256,2304]{1,0:T(8,128)(2,1)} async-done(((bf16[256,2304]{1,0:T(8,128)(2,1)}), bf16[256,2304]{1,0:T(8,128)(2,1)}) %all-reduce.2.cloned.1.call-update) | async-done | bytes 1179664 | tf_op jit(solution)/shard_map/psum | solution.py:88
  171.9 3.6 convert_add_fusion
  176.6 74.4 %all_to_all.15 = bf16[8,80,2304]{2,1,0:T(8,128)(2,1)S(1)} all-to-all(bf16[8,80,2304]{2,1,0:T(8,128)(2,1)S(1)} %convolution_convert_fusion.1), channel_id=1, replica_groups=mesh['ry'=4,'rxz'=8,'tp'=8] {'rxz'}, dimensions={0} | all-to-all | bytes 5898240 | tf_op jit(solution)/shard_map/all_to_all | solution.py:108
  251.1 1.6 copy-done.5
  252.7 4.0 %fusion.5 = f32[640,720]{0,1:T(8,128)} fusion(bf16[640,2304]{1,0:T(8,128)(2,1)S(1)} %bitcast.65, bf16[1,2304,720]{1,2,0:T(8,128)(2,1)S(1)} %copy-done.9), kind=kOutput, calls=%fused_computation.11 | convolution fusion | flops 2123366400 | bytes 8110080 | tf_op jit(solution)/shard_map/dot_general | solution.py:110
  256.7 14.5 %convolution_convert_fusion = bf16[640,2304]{1,0:T(8,128)(2,1)} fusion(bf16[1,720,2304]{2,1,0:T(8,128)(2,1)S(1)} %copy-done, f32[640,720]{0,1:T(8,128)} %fusion.5, bf16[640,2304]{1,0:T(8,128)(2,1)} %bitcast.66, bf16[1,2304,720]{1,2,0:T(8,128)(2,1)} %param.28), kind=kOutput, calls=%fused_computation.3 | convolution fusion | flops 4250972160 | bytes 14376960 | tf_op jit(solution)/shard_map/dot_general | solution.py:113
  271.2 7.4 %all-to-all-start.2 = ((bf16[8,80,2304]{2,1,0:T(8,128)(2,1)}), bf16[8,80,2304]{2,1,0:T(8,128)(2,1)}, u32[]{:S(2)}, u32[]{:S(2)}) async-start(bf16[8,80,2304]{2,1,0:T(8,128)(2,1)} %bitcast.64), calls=%async_computation.2 | async-start | bytes 5898240 | tf_op jit(solution)/shard_map/all_to_all | solution.py:114
  278.6 2.2 select_reduce_fusion.1
  280.8 57.1 %all-to-all-done.2 = bf16[8,80,2304]{2,1,0:T(8,128)(2,1)} async-done(((bf16[8,80,2304]{2,1,0:T(8,128)(2,1)}), bf16[8,80,2304]{2,1,0:T(8,128)(2,1)}, u32[]{:S(2)}, u32[]{:S(2)}) %all-to-all-start.2) | async-done | bytes 2949152 | tf_op jit(solution)/shard_map/all_to_all | solution.py:114
  337.9 6.4 %fusion.1 = bf16[2304,256]{1,0:T(8,128)(2,1)} fusion(bf16[8,80,2304]{2,1,0:T(8,128)(2,1)} %all-to-all-done.2, f32[8,256]{1,0:T(8,128)S(1)} %select_add_fusion, s32[8,256]{1,0:T(8,128)S(1)} %add_bitcast_fusion, pred[8,256]{1,0:T(8,128)(4,1)S(1)} %fusion.24), kind=kOutput, calls=%fused_computation.7 | convolution fusion | flops 4530929664 | bytes 4147200 | tf_op jit(solution)/shard_map/est,esd->td/dot_general | solution.py:125
  344.3 39.9 %reduce-scatter.4.cloned.1.call-done = bf16[288,256]{1,0:T(8,128)(2,1)} async-done(((bf16[2304,256]{1,0:T(8,128)(2,1)}), bf16[288,256]{1,0:T(8,128)(2,1)}) %reduce-scatter.4.cloned.1.call-update) | async-done | bytes 147472
  385.3 1.9 add_convert_fusion
  387.2 1.7 copy.33
  (64 shorter events, 11.8 us)
Async XLA Ops:
  6.5 250.1 %copy-start = (bf16[1,720,2304]{2,1,0:T(8,128)(2,1)S(1)}, bf16[1,720,2304]{2,1,0:T(8,128)(2,1)}, u32[]{:S(2)}) copy-start(bf16[1,720,2304]{2,1,0:T(8,128)(2,1)} %param.29) | copy-start | bytes 9953284
  6.5 18.1 %copy-start.11 = (s32[1,4]{1,0:T(1,128)S(1)}, s32[1,4]{1,0:T(1,128)}, u32[]{:S(2)}) copy-start(s32[1,4]{1,0:T(1,128)} %param.22) | copy-start | bytes 52
  6.5 18.3 %copy-start.12 = (s32[1,4]{1,0:T(1,128)S(1)}, s32[1,4]{1,0:T(1,128)}, u32[]{:S(2)}) copy-start(s32[1,4]{1,0:T(1,128)} %param.23) | copy-start | bytes 52
  6.5 18.3 %copy-start.1 = (s32[16]{0:T(128)S(1)}, s32[16]{0:T(128)}, u32[]{:S(2)}) copy-start(s32[16]{0:T(128)} %param.21) | copy-start | bytes 196
  6.5 19.0 %copy-start.2 = (s32[64]{0:T(128)S(1)}, s32[64]{0:T(128)}, u32[]{:S(2)}) copy-start(s32[64]{0:T(128)} %param.20) | copy-start | bytes 772
  8.7 17.6 %copy-start.6 = (bf16[256,288]{0,1:T(8,128)(2,1)S(1)}, bf16[256,288]{0,1:T(8,128)(2,1)}, u32[]{:S(2)}) copy-start(bf16[256,288]{0,1:T(8,128)(2,1)} %param.16) | copy-start | bytes 442372
  10.4 44.3 %all-to-all-start = ((bf16[32,2,9216]{2,1,0:T(2,128)(2,1)}), bf16[32,2,9216]{2,1,0:T(2,128)(2,1)}, u32[]{:S(2)}, u32[]{:S(2)}) async-start(bf16[32,2,9216]{2,1,0:T(2,128)(2,1)} %stack.2), calls=%async_computation | async-start | bytes 2359296 | tf_op jit(solution)/shard_map/all_to_all | solution.py:65
  24.6 147.2 %all-reduce.2.cloned.1.call-start = ((), (), s32[]{:S(2)}) async-start(), calls=%async_computation.4 | async-start | bytes 2359296 | tf_op jit(solution)/shard_map/psum | solution.py:88
  97.9 2.8 copy-start.8
  97.9 3.7 copy-start.7
  171.9 3.6 copy-start.3
  171.9 3.6 copy-start.4
  176.6 76.1 %copy-start.9 = (bf16[1,2304,720]{1,2,0:T(8,128)(2,1)S(1)}, bf16[1,2304,720]{1,2,0:T(8,128)(2,1)}, u32[]{:S(2)}) copy-start(bf16[1,2304,720]{1,2,0:T(8,128)(2,1)} %param.27) | copy-start | bytes 9953284
  251.1 1.6 copy-start.5
  271.2 7.4 %copy-start.10 = (bf16[2304,8]{0,1:T(8,128)(2,1)S(1)}, bf16[2304,8]{0,1:T(8,128)(2,1)}, u32[]{:S(2)}) copy-start(bf16[2304,8]{0,1:T(8,128)(2,1)} %param.25) | copy-start | bytes 110596
  271.2 66.7 %all-to-all-start.2 = ((bf16[8,80,2304]{2,1,0:T(8,128)(2,1)}), bf16[8,80,2304]{2,1,0:T(8,128)(2,1)}, u32[]{:S(2)}, u32[]{:S(2)}) async-start(bf16[8,80,2304]{2,1,0:T(8,128)(2,1)} %bitcast.64), calls=%async_computation.2 | async-start | bytes 5898240 | tf_op jit(solution)/shard_map/all_to_all | solution.py:114
  278.5 105.7 %reduce-scatter.4.cloned.1.call-start = ((), (), s32[]{:S(2)}) async-start(), calls=%async_computation.5 | async-start | bytes 1327104
Sparse Core Ops, SparseCore 0:
  100.9 70.9 all-reduce.1
  344.5 39.7 reduce-scatter.3
